TPU v7x, 32 devices: a whole 2x2x4 slice. The times are simulated.
32 devices in a mesh: energy: 4 (over x, core), slab: 8 (over z, y).
Axes of the slice: x: 2, y: 2, z: 4, core: 2. Of those that a mesh axis runs over, the one named last changes fastest.
Arguments:
- g_lesser: bfloat16 [4, 8, 3, 2, 256, 256], P('energy', 'slab'), may hold values from -6 to 6
- g_greater: bfloat16 [4, 8, 3, 2, 256, 256], P('energy', 'slab'), may hold values from -6 to 6
- v_diag: bfloat16 [8, 2, 256, 256], P('slab'), may hold values from -0.15625 to 0.15625
- v_upper: bfloat16 [8, 2, 256, 256], P('slab'), may hold values from -0.15625 to 0.15625
Outputs:
- w_diag: bfloat16 [4, 8, 2, 256, 256], P('energy', 'slab')
- w_upper: bfloat16 [4, 8, 2, 256, 256], P('energy', 'slab')
All inputs are finite; a program needn't handle non-finite values.
Results may differ from a plain program's by a relative error of at most 0.0058.
Values may be sent and summed in bfloat16 or wider, within the bound.
No kernel may reach another device: no remote copies, remote signals or barrier semaphores. Data moves between devices by JAX's collectives and lax.ppermute only.
A program may use at most 64 MiB of HBM per device.

v0:
```python
import math
import jax
import jax.numpy as jnp
from jax import lax
from jax.sharding import PartitionSpec as P


def extended(shard, sides, width):
    for axis, dim in sides:
        count, length = (lax.axis_size(axis), shard.shape[dim])
        up = [(i, (i + 1) % count) for i in range(count - 1)]
        down = [(j, i) for i, j in up]
        last = lax.slice_in_dim(shard, length - width, length, axis=dim)
        initial = lax.slice_in_dim(shard, 0, width, axis=dim)
        before = lax.ppermute(last, axis, up)
        after = lax.ppermute(initial, axis, down)
        shard = jnp.concatenate([before, shard, after], axis=dim)
    return shard


def passed_along(value, axis, steps):
    count = lax.axis_size(axis)
    initial, last = (max(0, -steps), min(count, count - steps))
    return lax.ppermute(value, axis, [(source, source + steps) for source in range(initial, last)])


def complex_product(left_block, right_block, left_adjoint=False, right_adjoint=False):
    left_re = left_block[..., 0, :, :]
    left_im = left_block[..., 1, :, :]
    right_re = right_block[..., 0, :, :]
    right_im = right_block[..., 1, :, :]
    pattern = (
        ("...ji" if left_adjoint else "...ij")
        + ","
        + ("...kj" if right_adjoint else "...jk")
        + "->...ik"
    )

    def contract(first_part, second_part):
        return jnp.einsum(pattern, first_part, second_part, preferred_element_type=jnp.float32)

    left_sign = -1.0 if left_adjoint else 1.0
    right_sign = -1.0 if right_adjoint else 1.0
    real_part = contract(left_re, right_re) - left_sign * right_sign * contract(left_im, right_im)
    imag_part = right_sign * contract(left_re, right_im) + left_sign * contract(left_im, right_re)
    return jnp.stack([real_part, imag_part], axis=-3)


def transform(table, signal):
    return jnp.einsum("fn,n...->f...", table, signal, precision=lax.Precision.HIGH)


def correlate(pieces):
    lesser, greater = pieces
    energies = lesser.shape[0]
    length = 2 * energies
    frequency = jnp.arange(length, dtype=jnp.int32)
    energy_ids = jnp.arange(energies, dtype=jnp.int32)
    step_angle = 2.0 * math.pi / length
    forward_angle = (frequency[:, None] * energy_ids[None, :] % length).astype(
        jnp.float32
    ) * step_angle
    shifts = energy_ids - energies // 2
    inverse_angle = (shifts[:, None] * frequency[None, :] % length).astype(jnp.float32) * step_angle
    forward_cos = jnp.cos(forward_angle)
    forward_sin = jnp.sin(forward_angle)
    inverse_cos = jnp.cos(inverse_angle)
    inverse_sin = jnp.sin(inverse_angle)

    def spectrum(signal):
        signal_re = signal[:, :, :, 0].astype(jnp.float32)
        signal_im = signal[:, :, :, 1].astype(jnp.float32)
        spec_re = transform(forward_cos, signal_re) + transform(forward_sin, signal_im)
        spec_im = transform(forward_cos, signal_im) - transform(forward_sin, signal_re)
        return (spec_re, spec_im)

    lesser_re, lesser_im = spectrum(lesser)
    greater_re, greater_im = spectrum(greater)
    cross_re = lesser_re * greater_re + lesser_im * greater_im
    cross_im = lesser_im * greater_re - lesser_re * greater_im
    corr_re = (transform(inverse_cos, cross_re) - transform(inverse_sin, cross_im)) / length
    corr_im = (transform(inverse_cos, cross_im) + transform(inverse_sin, cross_re)) / length
    factor = 1.0 / math.sqrt(energies)
    polar_entries = jnp.stack([-corr_im * factor, corr_re * factor], axis=3).astype(jnp.bfloat16)
    return lax.all_to_all(polar_entries, "energy", split_axis=0, concat_axis=4, tiled=True)


def per_device(g_lesser, g_greater, v_diag, v_upper):
    local_rows = v_diag.shape[0]
    total_rows = local_rows * lax.axis_size("slab")
    first_row = lax.axis_index("slab") * local_rows
    inside = first_row + jnp.arange(local_rows, dtype=jnp.int32) < total_rows - 1
    inside = inside.astype(jnp.bfloat16)[:, None, None, None]
    coupling = jnp.stack([v_diag, v_upper * inside], axis=1)
    padded = extended(coupling, (("slab", 0),), 1)
    diag_below = padded[:-2, 0][None]
    diag_middle = padded[1:-1, 0][None]
    diag_above = padded[2:, 0][None]
    upper_below = padded[:-2, 1][None]
    upper_middle = padded[1:-1, 1][None]
    upper_above = padded[2:, 1][None]
    middle = correlate(
        (
            lax.all_to_all(g_lesser, "energy", split_axis=4, concat_axis=0, tiled=True),
            lax.all_to_all(g_greater, "energy", split_axis=4, concat_axis=0, tiled=True),
        )
    )
    toward_above_y = complex_product(middle[:, :, 1], upper_middle) + complex_product(
        middle[:, :, 2], diag_above
    )
    toward_above_z = complex_product(middle[:, :, 2], upper_above)
    toward_below_y = complex_product(middle[:, :, 0], diag_below) + complex_product(
        middle[:, :, 1], upper_below, False, True
    )
    toward_below_z = (
        complex_product(middle[:, :, 0], upper_below)
        + complex_product(middle[:, :, 1], diag_middle)
        + complex_product(middle[:, :, 2], upper_middle, False, True)
    )
    sent_up = jnp.stack([toward_above_y, toward_above_z], axis=2).astype(jnp.bfloat16)
    sent_down = jnp.stack([toward_below_y, toward_below_z], axis=2).astype(jnp.bfloat16)
    arrived_below = passed_along(sent_up[:, -1:], "slab", 1)
    from_below = jnp.concatenate([arrived_below, sent_up[:, :-1]], axis=1)
    arrived_above = passed_along(sent_down[:, :1], "slab", -1)
    from_above = jnp.concatenate([sent_down[:, 1:], arrived_above], axis=1)
    below_y = from_below[:, :, 0]
    below_z = from_below[:, :, 1]
    above_y = from_above[:, :, 0]
    above_z = from_above[:, :, 1]
    middle_y = (
        complex_product(middle[:, :, 0], upper_below)
        + complex_product(middle[:, :, 1], diag_middle)
        + complex_product(middle[:, :, 2], upper_middle, False, True)
    ).astype(jnp.bfloat16)
    middle_z = (
        complex_product(middle[:, :, 1], upper_middle)
        + complex_product(middle[:, :, 2], diag_above)
    ).astype(jnp.bfloat16)
    w_diag = (
        complex_product(upper_below, below_y, True, False)
        + complex_product(diag_middle, middle_y)
        + complex_product(upper_middle, above_y)
    ).astype(jnp.bfloat16)
    w_upper = (
        complex_product(upper_below, below_z, True, False)
        + complex_product(diag_middle, middle_z)
        + complex_product(upper_middle, above_z)
    ).astype(jnp.bfloat16)
    return (w_diag, w_upper)


def solution(mesh):
    placed = (
        P("energy", "slab", None, None, None, None),
        P("energy", "slab", None, None, None, None),
        P("slab", None, None, None),
        P("slab", None, None, None),
    )
    return jax.shard_map(
        per_device,
        mesh=mesh,
        in_specs=placed,
        out_specs=(P("energy", "slab", None, None, None), P("energy", "slab", None, None, None)),
        check_vma=False,
    )
```

profile of v0, /device:TPU:26, one launch (start us, length us, event | category | flops | bytes accessed | tf_op | source)
XLA Modules:
  0.0 119.2 jit_solution(980924947038684042)
XLA Ops:
  0.6 2.9 %copy.44 = bf16[1,1,3,2,256,256]{5,2,3,1,0,4:T(4,128)(2,1)} copy(bf16[1,1,3,2,256,256]{5,4,3,2,1,0:T(8,128)(2,1)} %param.5) | data formatting | bytes 1572864 | tf_op args[1]
  3.5 4.0 %all-to-all-start.1 = ((bf16[1,1,3,2,256,256]{5,2,3,1,0,4:T(4,128)(2,1)}), bf16[1,1,3,2,256,256]{5,2,3,1,0,4:T(4,128)(2,1)S(1)}, u32[]{:S(2)}, u32[]{:S(2)}) async-start(bf16[1,1,3,2,256,256]{5,2,3,1,0,4:T(4,128)(2,1)} %copy.44), calls=%async_computation.1 | async-start | bytes 2097152 | tf_op jit(solution)/shard_map/all_to_all | solution.py:105
  7.5 1.7 %copy.41 = bf16[1,1,3,2,256,256]{5,2,3,1,0,4:T(4,128)(2,1)} copy(bf16[1,1,3,2,256,256]{5,4,3,2,1,0:T(8,128)(2,1)S(1)} %copy-done.2) | data formatting | bytes 1572864 | tf_op args[0]
  9.2 11.1 %all-to-all-done.1 = bf16[1,1,3,2,256,256]{5,2,3,1,0,4:T(4,128)(2,1)S(1)} async-done(((bf16[1,1,3,2,256,256]{5,2,3,1,0,4:T(4,128)(2,1)}), bf16[1,1,3,2,256,256]{5,2,3,1,0,4:T(4,128)(2,1)S(1)}, u32[]{:S(2)}, u32[]{:S(2)}) %all-to-all-start.1) | async-done | bytes 786464 | tf_op jit(solution)/shard_map/all_to_all | solution.py:105
  20.3 5.1 %all-to-all-start = ((bf16[1,1,3,2,256,256]{5,2,3,1,0,4:T(4,128)(2,1)}), bf16[1,1,3,2,256,256]{5,2,3,1,0,4:T(4,128)(2,1)S(1)}, u32[]{:S(2)}, u32[]{:S(2)}) async-start(bf16[1,1,3,2,256,256]{5,2,3,1,0,4:T(4,128)(2,1)} %copy.41), calls=%async_computation | async-start | bytes 2097152 | tf_op jit(solution)/shard_map/all_to_all | solution.py:104
  26.2 1.9 %fusion.43 = f32[8,3,64,256]{3,0,2,1:T(8,128)} fusion(bf16[4,1,3,2,64,256]{5,0,4,2,3,1:T(4,128)(2,1)S(1)} %bitcast.359), kind=kOutput, calls=%fused_computation.102 | convolution fusion | flops 9437632 | bytes 1966080 | tf_op jit(solution)/shard_map/fn,n...->f.../dot_general | solution.py:50
  28.8 9.4 %all-to-all-done = bf16[1,1,3,2,256,256]{5,2,3,1,0,4:T(4,128)(2,1)S(1)} async-done(((bf16[1,1,3,2,256,256]{5,2,3,1,0,4:T(4,128)(2,1)}), bf16[1,1,3,2,256,256]{5,2,3,1,0,4:T(4,128)(2,1)S(1)}, u32[]{:S(2)}, u32[]{:S(2)}) %all-to-all-start) | async-done | bytes 786464 | tf_op jit(solution)/shard_map/all_to_all | solution.py:104
  42.1 0.8 convolution_subtract_fusion
  42.9 1.2 %multiply_subtract_fusion = (f32[8,3,64,256]{3,0,2,1:T(8,128)S(1)}, f32[8,3,64,256]{3,0,2,1:T(8,128)S(1)}) fusion(f32[8,3,64,256]{3,0,2,1:T(8,128)S(1)} %convolution_subtract_fusion, f32[8,3,64,256]{3,0,2,1:T(8,128)S(1)} %convolution_subtract_fusion.1, f32[8,3,64,256]{3,0,2,1:T(8,128)S(1)} %convolution_add_fusion.1, f32[8,3,64,256]{3,0,2,1:T(8,128)S(1)} %fusion.42, ...), kind=kOutput, calls=%fused_computation.1 | convolution fusion | flops 12190144 | bytes 9830400 | tf_op jit(solution)/shard_map/fn,n...->f.../dot_general | solution.py:50
  44.1 0.9 fusion.80
  45.0 0.9 fusion.78
  45.9 1.1 fusion.7
  46.9 1.0 fusion.6
  48.5 1.0 copy.47
  49.6 5.1 %all-to-all-start.2 = ((bf16[4,1,3,2,64,256]{5,4,2,3,1,0:T(8,128)(2,1)}), bf16[4,1,3,2,64,256]{5,4,2,3,1,0:T(8,128)(2,1)S(1)}, u32[]{:S(2)}, u32[]{:S(2)}) async-start(bf16[4,1,3,2,64,256]{5,4,2,3,1,0:T(8,128)(2,1)} %copy.47), calls=%async_computation.2 | async-start | bytes 1572864 | tf_op jit(solution)/shard_map/all_to_all | solution.py:85
  54.8 3.6 %collective-permute-start = (bf16[1,2,2,256,256]{4,3,2,1,0:T(8,128)(2,1)S(1)}, bf16[1,2,2,256,256]{4,3,2,1,0:T(8,128)(2,1)S(1)}, u32[]{:S(2)}, u32[]{:S(2)}) collective-permute-start(bf16[1,2,2,256,256]{4,3,2,1,0:T(8,128)(2,1)S(1)} %pad_maximum_fusion.1), channel_id=1, source_target_pairs={{0,1},{1,2},{2,3},{3,4},{4,5},{5,6},{6,7},{8,9},{9,10},{10,11},{11... | collective-permute-start | bytes 1572872 | tf_op jit(solution)/shard_map/ppermute | solution.py:15
  58.4 3.3 %collective-permute-start.1 = (bf16[1,2,2,256,256]{4,3,2,1,0:T(8,128)(2,1)S(1)}, bf16[1,2,2,256,256]{4,3,2,1,0:T(8,128)(2,1)S(1)}, u32[]{:S(2)}, u32[]{:S(2)}) collective-permute-start(bf16[1,2,2,256,256]{4,3,2,1,0:T(8,128)(2,1)S(1)} %pad_maximum_fusion.1), channel_id=1, source_target_pairs={{1,0},{2,1},{3,2},{4,3},{5,4},{6,5},{7,6},{9,8},{10,9},{11,10},{12... | collective-permute-start | bytes 1572872 | tf_op jit(solution)/shard_map/ppermute | solution.py:16
  61.7 3.0 %all-to-all-done.2 = bf16[4,1,3,2,64,256]{5,4,2,3,1,0:T(8,128)(2,1)S(1)} async-done(((bf16[4,1,3,2,64,256]{5,4,2,3,1,0:T(8,128)(2,1)}), bf16[4,1,3,2,64,256]{5,4,2,3,1,0:T(8,128)(2,1)S(1)}, u32[]{:S(2)}, u32[]{:S(2)}) %all-to-all-start.2) | async-done | bytes 786464 | tf_op jit(solution)/shard_map/all_to_all | solution.py:85
  66.8 15.9 %collective-permute-done.1 = bf16[1,2,2,256,256]{4,3,2,1,0:T(8,128)(2,1)S(1)} collective-permute-done((bf16[1,2,2,256,256]{4,3,2,1,0:T(8,128)(2,1)S(1)}, bf16[1,2,2,256,256]{4,3,2,1,0:T(8,128)(2,1)S(1)}, u32[]{:S(2)}, u32[]{:S(2)}) %collective-permute-start.1) | collective-permute-done | bytes 524320 | tf_op jit(solution)/shard_map/ppermute | solution.py:16
  87.1 1.9 %collective-permute-start.3 = (bf16[1,1,2,2,256,256]{5,4,3,2,1,0:T(8,128)(2,1)S(1)}, bf16[1,1,2,2,256,256]{5,4,3,2,1,0:T(8,128)(2,1)S(1)}, u32[]{:S(2)}, u32[]{:S(2)}) collective-permute-start(bf16[1,1,2,2,256,256]{5,4,3,2,1,0:T(8,128)(2,1)S(1)} %pad_maximum_fusion.3), channel_id=1, source_target_pairs={{1,0},{2,1},{3,2},{4,3},{5,4},{6,5},{7,6},{9,8},{10,9},{11,10},{12... | collective-permute-start | bytes 1572872 | tf_op jit(solution)/shard_map/ppermute | solution.py:24
  90.3 3.9 %collective-permute-start.2 = (bf16[1,1,2,2,256,256]{5,4,3,2,1,0:T(8,128)(2,1)S(1)}, bf16[1,1,2,2,256,256]{5,4,3,2,1,0:T(8,128)(2,1)S(1)}, u32[]{:S(2)}, u32[]{:S(2)}) collective-permute-start(bf16[1,1,2,2,256,256]{5,4,3,2,1,0:T(8,128)(2,1)S(1)} %pad_maximum_fusion.2), channel_id=1, source_target_pairs={{0,1},{1,2},{2,3},{3,4},{4,5},{5,6},{6,7},{8,9},{9,10},{10,11},{11... | collective-permute-start | bytes 1572872 | tf_op jit(solution)/shard_map/ppermute | solution.py:24
  95.2 18.9 %collective-permute-done.3 = bf16[1,1,2,2,256,256]{5,4,3,2,1,0:T(8,128)(2,1)S(1)} collective-permute-done((bf16[1,1,2,2,256,256]{5,4,3,2,1,0:T(8,128)(2,1)S(1)}, bf16[1,1,2,2,256,256]{5,4,3,2,1,0:T(8,128)(2,1)S(1)}, u32[]{:S(2)}, u32[]{:S(2)}) %collective-permute-start.3) | collective-permute-done | bytes 524320 | tf_op jit(solution)/shard_map/ppermute | solution.py:24
  116.7 0.8 fusion.39
  118.4 0.8 fusion.32
  (88 shorter events, 17.7 us)
Async XLA Ops:
  0.6 6.9 %copy-start.2 = (bf16[1,1,3,2,256,256]{5,4,3,2,1,0:T(8,128)(2,1)S(1)}, bf16[1,1,3,2,256,256]{5,4,3,2,1,0:T(8,128)(2,1)}, u32[]{:S(2)}) copy-start(bf16[1,1,3,2,256,256]{5,4,3,2,1,0:T(8,128)(2,1)} %param.4) | copy-start | bytes 2359300
  3.5 16.8 %all-to-all-start.1 = ((bf16[1,1,3,2,256,256]{5,2,3,1,0,4:T(4,128)(2,1)}), bf16[1,1,3,2,256,256]{5,2,3,1,0,4:T(4,128)(2,1)S(1)}, u32[]{:S(2)}, u32[]{:S(2)}) async-start(bf16[1,1,3,2,256,256]{5,2,3,1,0,4:T(4,128)(2,1)} %copy.44), calls=%async_computation.1 | async-start | bytes 2097152 | tf_op jit(solution)/shard_map/all_to_all | solution.py:105
  20.3 17.9 %all-to-all-start = ((bf16[1,1,3,2,256,256]{5,2,3,1,0,4:T(4,128)(2,1)}), bf16[1,1,3,2,256,256]{5,2,3,1,0,4:T(4,128)(2,1)S(1)}, u32[]{:S(2)}, u32[]{:S(2)}) async-start(bf16[1,1,3,2,256,256]{5,2,3,1,0,4:T(4,128)(2,1)} %copy.41), calls=%async_computation | async-start | bytes 2097152 | tf_op jit(solution)/shard_map/all_to_all | solution.py:104
  39.0 1.5 %copy-start.1 = (f32[8,3,64,256]{3,0,2,1:T(8,128)S(1)}, f32[8,3,64,256]{3,0,2,1:T(8,128)}, u32[]{:S(2)}) copy-start(f32[8,3,64,256]{3,0,2,1:T(8,128)} %fusion.43) | copy-start | bytes 4718596
  48.5 6.2 %copy-start.3 = (bf16[1,2,256,256]{3,2,1,0:T(8,128)(2,1)S(1)}, bf16[1,2,256,256]{3,2,1,0:T(8,128)(2,1)}, u32[]{:S(2)}) copy-start(bf16[1,2,256,256]{3,2,1,0:T(8,128)(2,1)} %param.7) | copy-start | bytes 786436
  48.5 6.2 %copy-start = (bf16[1,2,256,256]{3,2,1,0:T(8,128)(2,1)S(1)}, bf16[1,2,256,256]{3,2,1,0:T(8,128)(2,1)}, u32[]{:S(2)}) copy-start(bf16[1,2,256,256]{3,2,1,0:T(8,128)(2,1)} %param.6) | copy-start | bytes 786436
  49.6 15.1 %all-to-all-start.2 = ((bf16[4,1,3,2,64,256]{5,4,2,3,1,0:T(8,128)(2,1)}), bf16[4,1,3,2,64,256]{5,4,2,3,1,0:T(8,128)(2,1)S(1)}, u32[]{:S(2)}, u32[]{:S(2)}) async-start(bf16[4,1,3,2,64,256]{5,4,2,3,1,0:T(8,128)(2,1)} %copy.47), calls=%async_computation.2 | async-start | bytes 1572864 | tf_op jit(solution)/shard_map/all_to_all | solution.py:85
  54.8 29.6 %collective-permute-start = (bf16[1,2,2,256,256]{4,3,2,1,0:T(8,128)(2,1)S(1)}, bf16[1,2,2,256,256]{4,3,2,1,0:T(8,128)(2,1)S(1)}, u32[]{:S(2)}, u32[]{:S(2)}) collective-permute-start(bf16[1,2,2,256,256]{4,3,2,1,0:T(8,128)(2,1)S(1)} %pad_maximum_fusion.1), channel_id=1, source_target_pairs={{0,1},{1,2},{2,3},{3,4},{4,5},{5,6},{6,7},{8,9},{9,10},{10,11},{11... | collective-permute-start | bytes 1572872 | tf_op jit(solution)/shard_map/ppermute | solution.py:15
  58.4 24.4 %collective-permute-start.1 = (bf16[1,2,2,256,256]{4,3,2,1,0:T(8,128)(2,1)S(1)}, bf16[1,2,2,256,256]{4,3,2,1,0:T(8,128)(2,1)S(1)}, u32[]{:S(2)}, u32[]{:S(2)}) collective-permute-start(bf16[1,2,2,256,256]{4,3,2,1,0:T(8,128)(2,1)S(1)} %pad_maximum_fusion.1), channel_id=1, source_target_pairs={{1,0},{2,1},{3,2},{4,3},{5,4},{6,5},{7,6},{9,8},{10,9},{11,10},{12... | collective-permute-start | bytes 1572872 | tf_op jit(solution)/shard_map/ppermute | solution.py:16
  87.1 27.0 %collective-permute-start.3 = (bf16[1,1,2,2,256,256]{5,4,3,2,1,0:T(8,128)(2,1)S(1)}, bf16[1,1,2,2,256,256]{5,4,3,2,1,0:T(8,128)(2,1)S(1)}, u32[]{:S(2)}, u32[]{:S(2)}) collective-permute-start(bf16[1,1,2,2,256,256]{5,4,3,2,1,0:T(8,128)(2,1)S(1)} %pad_maximum_fusion.3), channel_id=1, source_target_pairs={{1,0},{2,1},{3,2},{4,3},{5,4},{6,5},{7,6},{9,8},{10,9},{11,10},{12... | collective-permute-start | bytes 1572872 | tf_op jit(solution)/shard_map/ppermute | solution.py:24
  90.3 25.3 %collective-permute-start.2 = (bf16[1,1,2,2,256,256]{5,4,3,2,1,0:T(8,128)(2,1)S(1)}, bf16[1,1,2,2,256,256]{5,4,3,2,1,0:T(8,128)(2,1)S(1)}, u32[]{:S(2)}, u32[]{:S(2)}) collective-permute-start(bf16[1,1,2,2,256,256]{5,4,3,2,1,0:T(8,128)(2,1)S(1)} %pad_maximum_fusion.2), channel_id=1, source_target_pairs={{0,1},{1,2},{2,3},{3,4},{4,5},{5,6},{6,7},{8,9},{9,10},{10,11},{11... | collective-permute-start | bytes 1572872 | tf_op jit(solution)/shard_map/ppermute | solution.py:24
where the time goes:
time: 120 us; the launch traced here: 119 us
  waiting for transfers between devices  58.3 us (49%)
  starting transfers between devices  27 us (22%)
  matrix products  22.5 us (19%)
  local copies, waits for them, and re-layouts  7.24 us (6%)
  other arithmetic  2.8 us (2%)
  between operations  1.33 us (1%)
    ppermute x2, waiting for transfers between devices, passed_along(): lax.ppermute(value, axis, [(source, source + steps) for source in range(i...  18.9 us
    ppermute x1, waiting for transfers between devices, extended(): after = lax.ppermute(initial, axis, down)  15.9 us
    dot_general x12, matrix products, transform(): jnp.einsum('fn,n...->f...', table, signal, precision=lax.Precision.HIGH)  11.5 us
    all_to_all x1, waiting for transfers between devices, per_device(): lax.all_to_all(g_greater, 'energy', split_axis=4, concat_axis=0, tiled=True)  11.1 us
    dot_general x56, matrix products, contract(): jnp.einsum(pattern, first_part, second_part, preferred_element_type=jnp.f...  11 us
    all_to_all x1, waiting for transfers between devices, per_device(): lax.all_to_all(g_lesser, 'energy', split_axis=4, concat_axis=0, tiled=True)  9.39 us
    ppermute x2, starting transfers between devices, passed_along(): lax.ppermute(value, axis, [(source, source + steps) for source in range(i...  5.87 us
    all_to_all x1, starting transfers between devices, per_device(): lax.all_to_all(g_lesser, 'energy', split_axis=4, concat_axis=0, tiled=True)  5.12 us
  transfers between devices with their start and end apart: 7, of which 5 were waited for; matrix products, arithmetic and copies ran while one was open for 10% of the time, Pallas kernels for 0%

commit v1 on v0

--- a/solution.py
+++ b/solution.py
@@ -3,6 +3,28 @@
 import jax.numpy as jnp
 from jax import lax
 from jax.sharding import PartitionSpec as P
+
+
+def in_blocks(x, dim, size):
+    before, after = (x.shape[:dim], x.shape[dim + 1 :])
+    return jnp.moveaxis(x.reshape(*before, size, -1, *after), dim, 0)
+
+
+def joined_along(blocks, dim):
+    shape = list(blocks.shape[1:])
+    shape[dim] *= blocks.shape[0]
+    return jnp.moveaxis(blocks, 0, dim).reshape(shape)
+
+
+def exchange_directly(x, axis, split_dim, concat_dim):
+    devices, here = (lax.axis_size(axis), lax.axis_index(axis))
+    blocks = in_blocks(x, split_dim, devices)
+    outs = [blocks[here]]
+    for step in range(1, devices):
+        sent = blocks[(here + step) % devices]
+        outs.append(lax.ppermute(sent, axis, [(i, (i + step) % devices) for i in range(devices)]))
+    blocks = jnp.stack(outs)[(here - jnp.arange(devices)) % devices]
+    return joined_along(blocks, concat_dim)
 
 
 def extended(shard, sides, width):
@@ -102,7 +124,7 @@
     middle = correlate(
         (
             lax.all_to_all(g_lesser, "energy", split_axis=4, concat_axis=0, tiled=True),
-            lax.all_to_all(g_greater, "energy", split_axis=4, concat_axis=0, tiled=True),
+            exchange_directly(g_greater, "energy", 4, 0),
         )
     )
     toward_above_y = complex_product(middle[:, :, 1], upper_middle) + complex_product(

time: 120 us -> 105 us (0.88)
  waiting for transfers between devices: 58.3 us -> 47.1 us
  starting transfers between devices: 27 us -> 23.6 us
    all_to_all x1 -> x0, waiting for transfers between devices: 11.1 us -> none  [per_device(): lax.all_to_all(g_greater, 'energy', split_axis=4, concat_axis=0, tiled=True)]
    all_to_all x1 -> x0, starting transfers between devices: 4.02 us -> none  [per_device(): lax.all_to_all(g_greater, 'energy', split_axis=4, concat_axis=0, tiled=True)]
    unnamed x10 -> x9, local copies, waits for them, and re-layouts: 4.55 us -> 2.29 us
    ppermute x0 -> x3, starting transfers between devices: none -> 2.05 us  [exchange_directly(): lax.ppermute(sent, axis, [(i, (i + step) % devices) for i in range(device...]
    dynamic_slice x0 -> x1, local copies, waits for them, and re-layouts: none -> 1.34 us  [exchange_directly(): outs = [blocks[here]]]
    gather x0 -> x2, local copies, waits for them, and re-layouts: none -> 1.21 us  [exchange_directly(): blocks = jnp.stack(outs)[(here - jnp.arange(devices)) % devices]]
  transfers between devices with their start and end apart: 7 -> 9, of which waited for: 5 -> 5; matrix products, arithmetic and copies ran while one was open for 10% -> 13% of each run, Pallas kernels for 0% -> 0%
where the time goes in v1:
time: 105 us; the launch traced here: 104 us
  waiting for transfers between devices  47.1 us (45%)
  starting transfers between devices  23.6 us (22%)
  matrix products  22.5 us (21%)
  local copies, waits for them, and re-layouts  6.77 us (6%)
  other arithmetic  2.92 us (3%)
  between operations  1.42 us (1%)
    ppermute x2, waiting for transfers between devices, passed_along(): lax.ppermute(value, axis, [(source, source + steps) for source in range(i...  18.9 us
    ppermute x1, waiting for transfers between devices, extended(): after = lax.ppermute(initial, axis, down)  15.9 us
    dot_general x12, matrix products, transform(): jnp.einsum('fn,n...->f...', table, signal, precision=lax.Precision.HIGH)  11.5 us
    dot_general x56, matrix products, contract(): jnp.einsum(pattern, first_part, second_part, preferred_element_type=jnp.f...  11 us
    all_to_all x1, waiting for transfers between devices, per_device(): lax.all_to_all(g_lesser, 'energy', split_axis=4, concat_axis=0, tiled=True)  8.35 us
    ppermute x2, starting transfers between devices, passed_along(): lax.ppermute(value, axis, [(source, source + steps) for source in range(i...  5.87 us
    all_to_all x1, starting transfers between devices, per_device(): lax.all_to_all(g_lesser, 'energy', split_axis=4, concat_axis=0, tiled=True)  4.98 us
    all_to_all x1, starting transfers between devices, correlate(): lax.all_to_all(polar_entries, 'energy', split_axis=0, concat_axis=4, tile...  4 us
  transfers between devices with their start and end apart: 9, of which 5 were waited for; matrix products, arithmetic and copies ran while one was open for 13% of the time, Pallas kernels for 0%

profile of v1, /device:TPU:26, one launch (start us, length us, event | category | flops | bytes accessed | tf_op | source)
XLA Modules:
  0.0 104.4 jit_solution(4371863868725087674)
XLA Ops:
  0.7 1.3 %dynamic-slice_bitcast_fusion.3 = (bf16[1,1,1,3,2,64,256]{6,5,4,3,0,2,1:T(8,128)(2,1)S(1)}, bf16[1,1,3,2,64,256]{5,4,3,2,1,0:T(8,128)(2,1)S(1)}, bf16[1,1,3,2,64...) fusion(bf16[1,1,3,2,4,64,256]{6,5,4,3,2,1,0:T(8,128)(2,1)} %bitcast.406, s32[]{:T(128)S(6)} %select_n.84, ...), kind=kLoop, calls=%fused_computation.121 | loop fusion | bytes 1572880 | tf_op jit(solution)/shard_map/dynamic_slice | solution.py:22
  2.7 1.4 %collective-permute-start.3 = (bf16[1,1,3,2,64,256]{5,4,3,2,1,0:T(8,128)(2,1)S(1)}, bf16[1,1,3,2,64,256]{5,4,3,2,1,0:T(8,128)(2,1)S(1)}, u32[]{:S(2)}, u32[]{:S(2)}) collective-permute-start(bf16[1,1,3,2,64,256]{5,4,3,2,1,0:T(8,128)(2,1)S(1)} %get-tuple-element.10), channel_id=1, source_target_pairs={{0,24},{8,0},{16,8},{24,16},{1,25},{9,1},{17,9},{25,17},{2,26},{10... | collective-permute-start | bytes 589832 | tf_op jit(solution)/shard_map/ppermute | solution.py:25
  4.1 1.7 %copy.47 = bf16[1,1,3,2,256,256]{5,2,3,1,0,4:T(4,128)(2,1)} copy(bf16[1,1,3,2,256,256]{5,4,3,2,1,0:T(8,128)(2,1)S(1)} %copy-done.2) | data formatting | bytes 1572864 | tf_op args[0]
  5.7 5.0 %all-to-all-start = ((bf16[1,1,3,2,256,256]{5,2,3,1,0,4:T(4,128)(2,1)}), bf16[1,1,3,2,256,256]{5,2,3,1,0,4:T(4,128)(2,1)S(1)}, u32[]{:S(2)}, u32[]{:S(2)}) async-start(bf16[1,1,3,2,256,256]{5,2,3,1,0,4:T(4,128)(2,1)} %copy.47), calls=%async_computation | async-start | bytes 2097152 | tf_op jit(solution)/shard_map/all_to_all | solution.py:126
  10.8 0.9 collective-permute-done.3
  13.7 1.9 %fusion.44 = f32[8,3,64,256]{3,0,2,1:T(8,128)} fusion(bf16[4,1,3,2,64,256]{5,0,4,2,3,1:T(4,128)(2,1)S(1)} %bitcast.377), kind=kOutput, calls=%fused_computation.105 | convolution fusion | flops 9437632 | bytes 1966080 | tf_op jit(solution)/shard_map/fn,n...->f.../dot_general | solution.py:72
  16.4 8.3 %all-to-all-done = bf16[1,1,3,2,256,256]{5,2,3,1,0,4:T(4,128)(2,1)S(1)} async-done(((bf16[1,1,3,2,256,256]{5,2,3,1,0,4:T(4,128)(2,1)}), bf16[1,1,3,2,256,256]{5,2,3,1,0,4:T(4,128)(2,1)S(1)}, u32[]{:S(2)}, u32[]{:S(2)}) %all-to-all-start) | async-done | bytes 786464 | tf_op jit(solution)/shard_map/all_to_all | solution.py:126
  27.0 0.8 convolution_subtract_fusion.1
  29.2 1.2 %multiply_subtract_fusion = (f32[8,3,64,256]{3,0,2,1:T(8,128)S(1)}, f32[8,3,64,256]{3,0,2,1:T(8,128)S(1)}) fusion(f32[8,3,64,256]{3,0,2,1:T(8,128)S(1)} %convolution_add_fusion, f32[8,3,64,256]{3,0,2,1:T(8,128)S(1)} %convolution_subtract_fusion.1, f32[8,3,64,256]{3,0,2,1:T(8,128)S(1)} %convolution_add_fusion.1, f32[8,3,64,256]{3,0,2,1:T(8,128)S(1)} %copy-done.1, ...), kind=kOutput, calls=%fused_computation.2 | convolution fusion | flops 12190144 | bytes 9830400 | tf_op jit(solution)/shard_map/fn,n...->f.../dot_general | solution.py:72
  30.5 0.9 fusion.80
  31.3 0.9 fusion.78
  32.2 1.1 %fusion.7 = bf16[4,1,3,1,64,256]{5,0,4,2,3,1:T(4,128)(2,1)S(1)} fusion(f32[4,3,64,256]{3,0,2,1:T(4,128)S(1)} %fusion.80, f32[8,3,64,256]{3,0,2,1:T(8,128)S(1)} %get-tuple-element.3, s32[4]{0:T(128)S(1)} %iota_add_fusion), kind=kOutput, calls=%fused_computation.16 | convolution fusion | flops 10420672 | bytes 2752528 | tf_op jit(solution)/shard_map/fn,n...->f.../dot_general | solution.py:72
  33.3 1.0 fusion.6
  34.9 1.0 copy.55
  35.9 4.0 %all-to-all-start.1 = ((bf16[4,1,3,2,64,256]{5,4,2,3,1,0:T(8,128)(2,1)}), bf16[4,1,3,2,64,256]{5,4,2,3,1,0:T(8,128)(2,1)S(1)}, u32[]{:S(2)}, u32[]{:S(2)}) async-start(bf16[4,1,3,2,64,256]{5,4,2,3,1,0:T(8,128)(2,1)} %copy.55), calls=%async_computation.1 | async-start | bytes 1572864 | tf_op jit(solution)/shard_map/all_to_all | solution.py:107
  40.0 3.4 %collective-permute-start = (bf16[1,2,2,256,256]{4,3,2,1,0:T(8,128)(2,1)S(1)}, bf16[1,2,2,256,256]{4,3,2,1,0:T(8,128)(2,1)S(1)}, u32[]{:S(2)}, u32[]{:S(2)}) collective-permute-start(bf16[1,2,2,256,256]{4,3,2,1,0:T(8,128)(2,1)S(1)} %pad_maximum_fusion.1), channel_id=1, source_target_pairs={{0,1},{1,2},{2,3},{3,4},{4,5},{5,6},{6,7},{8,9},{9,10},{10,11},{11... | collective-permute-start | bytes 1572872 | tf_op jit(solution)/shard_map/ppermute | solution.py:37
  43.4 3.3 %collective-permute-start.4 = (bf16[1,2,2,256,256]{4,3,2,1,0:T(8,128)(2,1)S(1)}, bf16[1,2,2,256,256]{4,3,2,1,0:T(8,128)(2,1)S(1)}, u32[]{:S(2)}, u32[]{:S(2)}) collective-permute-start(bf16[1,2,2,256,256]{4,3,2,1,0:T(8,128)(2,1)S(1)} %pad_maximum_fusion.1), channel_id=1, source_target_pairs={{1,0},{2,1},{3,2},{4,3},{5,4},{6,5},{7,6},{9,8},{10,9},{11,10},{12... | collective-permute-start | bytes 1572872 | tf_op jit(solution)/shard_map/ppermute | solution.py:38
  46.8 3.1 %all-to-all-done.1 = bf16[4,1,3,2,64,256]{5,4,2,3,1,0:T(8,128)(2,1)S(1)} async-done(((bf16[4,1,3,2,64,256]{5,4,2,3,1,0:T(8,128)(2,1)}), bf16[4,1,3,2,64,256]{5,4,2,3,1,0:T(8,128)(2,1)S(1)}, u32[]{:S(2)}, u32[]{:S(2)}) %all-to-all-start.1) | async-done | bytes 786464 | tf_op jit(solution)/shard_map/all_to_all | solution.py:107
  52.1 15.9 %collective-permute-done.4 = bf16[1,2,2,256,256]{4,3,2,1,0:T(8,128)(2,1)S(1)} collective-permute-done((bf16[1,2,2,256,256]{4,3,2,1,0:T(8,128)(2,1)S(1)}, bf16[1,2,2,256,256]{4,3,2,1,0:T(8,128)(2,1)S(1)}, u32[]{:S(2)}, u32[]{:S(2)}) %collective-permute-start.4) | collective-permute-done | bytes 524320 | tf_op jit(solution)/shard_map/ppermute | solution.py:38
  72.3 1.9 %collective-permute-start.6 = (bf16[1,1,2,2,256,256]{5,4,3,2,1,0:T(8,128)(2,1)S(1)}, bf16[1,1,2,2,256,256]{5,4,3,2,1,0:T(8,128)(2,1)S(1)}, u32[]{:S(2)}, u32[]{:S(2)}) collective-permute-start(bf16[1,1,2,2,256,256]{5,4,3,2,1,0:T(8,128)(2,1)S(1)} %pad_maximum_fusion.3), channel_id=1, source_target_pairs={{1,0},{2,1},{3,2},{4,3},{5,4},{6,5},{7,6},{9,8},{10,9},{11,10},{12... | collective-permute-start | bytes 1572872 | tf_op jit(solution)/shard_map/ppermute | solution.py:46
  75.6 3.9 %collective-permute-start.5 = (bf16[1,1,2,2,256,256]{5,4,3,2,1,0:T(8,128)(2,1)S(1)}, bf16[1,1,2,2,256,256]{5,4,3,2,1,0:T(8,128)(2,1)S(1)}, u32[]{:S(2)}, u32[]{:S(2)}) collective-permute-start(bf16[1,1,2,2,256,256]{5,4,3,2,1,0:T(8,128)(2,1)S(1)} %pad_maximum_fusion.2), channel_id=1, source_target_pairs={{0,1},{1,2},{2,3},{3,4},{4,5},{5,6},{6,7},{8,9},{9,10},{10,11},{11... | collective-permute-start | bytes 1572872 | tf_op jit(solution)/shard_map/ppermute | solution.py:46
  80.5 18.9 %collective-permute-done.6 = bf16[1,1,2,2,256,256]{5,4,3,2,1,0:T(8,128)(2,1)S(1)} collective-permute-done((bf16[1,1,2,2,256,256]{5,4,3,2,1,0:T(8,128)(2,1)S(1)}, bf16[1,1,2,2,256,256]{5,4,3,2,1,0:T(8,128)(2,1)S(1)}, u32[]{:S(2)}, u32[]{:S(2)}) %collective-permute-start.6) | collective-permute-done | bytes 524320 | tf_op jit(solution)/shard_map/ppermute | solution.py:46
  101.9 0.8 fusion.39
  103.6 0.8 fusion.32
  (96 shorter events, 19.5 us)
Async XLA Ops:
  0.6 3.5 %copy-start.2 = (bf16[1,1,3,2,256,256]{5,4,3,2,1,0:T(8,128)(2,1)S(1)}, bf16[1,1,3,2,256,256]{5,4,3,2,1,0:T(8,128)(2,1)}, u32[]{:S(2)}) copy-start(bf16[1,1,3,2,256,256]{5,4,3,2,1,0:T(8,128)(2,1)} %param.4) | copy-start | bytes 2359300
  2.0 8.7 %collective-permute-start.1 = (bf16[1,1,3,2,64,256]{5,4,3,2,1,0:T(8,128)(2,1)S(1)}, bf16[1,1,3,2,64,256]{5,4,3,2,1,0:T(8,128)(2,1)S(1)}, u32[]{:S(2)}, u32[]{:S(2)}) collective-permute-start(bf16[1,1,3,2,64,256]{5,4,3,2,1,0:T(8,128)(2,1)S(1)} %get-tuple-element.9), channel_id=1, source_target_pairs={{0,8},{8,16},{16,24},{24,0},{1,9},{9,17},{17,25},{25,1},{2,10},{10... | collective-permute-start | bytes 589832 | tf_op jit(solution)/shard_map/ppermute | solution.py:25
  2.1 8.7 %collective-permute-start.2 = (bf16[1,1,3,2,64,256]{5,4,3,2,1,0:T(8,128)(2,1)S(1)}, bf16[1,1,3,2,64,256]{5,4,3,2,1,0:T(8,128)(2,1)S(1)}, u32[]{:S(2)}, u32[]{:S(2)}) collective-permute-start(bf16[1,1,3,2,64,256]{5,4,3,2,1,0:T(8,128)(2,1)S(1)} %get-tuple-element.8), channel_id=1, source_target_pairs={{0,16},{8,24},{16,0},{24,8},{1,17},{9,25},{17,1},{25,9},{2,18},{10... | collective-permute-start | bytes 589832 | tf_op jit(solution)/shard_map/ppermute | solution.py:25
  2.7 9.0 %collective-permute-start.3 = (bf16[1,1,3,2,64,256]{5,4,3,2,1,0:T(8,128)(2,1)S(1)}, bf16[1,1,3,2,64,256]{5,4,3,2,1,0:T(8,128)(2,1)S(1)}, u32[]{:S(2)}, u32[]{:S(2)}) collective-permute-start(bf16[1,1,3,2,64,256]{5,4,3,2,1,0:T(8,128)(2,1)S(1)} %get-tuple-element.10), channel_id=1, source_target_pairs={{0,24},{8,0},{16,8},{24,16},{1,25},{9,1},{17,9},{25,17},{2,26},{10... | collective-permute-start | bytes 589832 | tf_op jit(solution)/shard_map/ppermute | solution.py:25
  5.7 19.0 %all-to-all-start = ((bf16[1,1,3,2,256,256]{5,2,3,1,0,4:T(4,128)(2,1)}), bf16[1,1,3,2,256,256]{5,2,3,1,0,4:T(4,128)(2,1)S(1)}, u32[]{:S(2)}, u32[]{:S(2)}) async-start(bf16[1,1,3,2,256,256]{5,2,3,1,0,4:T(4,128)(2,1)} %copy.47), calls=%async_computation | async-start | bytes 2097152 | tf_op jit(solution)/shard_map/all_to_all | solution.py:126
  27.8 1.4 %copy-start.1 = (f32[8,3,64,256]{3,0,2,1:T(8,128)S(1)}, f32[8,3,64,256]{3,0,2,1:T(8,128)}, u32[]{:S(2)}) copy-start(f32[8,3,64,256]{3,0,2,1:T(8,128)} %fusion.44) | copy-start | bytes 4718596
  34.9 5.0 %copy-start.3 = (bf16[1,2,256,256]{3,2,1,0:T(8,128)(2,1)S(1)}, bf16[1,2,256,256]{3,2,1,0:T(8,128)(2,1)}, u32[]{:S(2)}) copy-start(bf16[1,2,256,256]{3,2,1,0:T(8,128)(2,1)} %param.7) | copy-start | bytes 786436
  34.9 5.1 %copy-start = (bf16[1,2,256,256]{3,2,1,0:T(8,128)(2,1)S(1)}, bf16[1,2,256,256]{3,2,1,0:T(8,128)(2,1)}, u32[]{:S(2)}) copy-start(bf16[1,2,256,256]{3,2,1,0:T(8,128)(2,1)} %param.6) | copy-start | bytes 786436
  35.9 14.0 %all-to-all-start.1 = ((bf16[4,1,3,2,64,256]{5,4,2,3,1,0:T(8,128)(2,1)}), bf16[4,1,3,2,64,256]{5,4,2,3,1,0:T(8,128)(2,1)S(1)}, u32[]{:S(2)}, u32[]{:S(2)}) async-start(bf16[4,1,3,2,64,256]{5,4,2,3,1,0:T(8,128)(2,1)} %copy.55), calls=%async_computation.1 | async-start | bytes 1572864 | tf_op jit(solution)/shard_map/all_to_all | solution.py:107
  40.0 29.6 %collective-permute-start = (bf16[1,2,2,256,256]{4,3,2,1,0:T(8,128)(2,1)S(1)}, bf16[1,2,2,256,256]{4,3,2,1,0:T(8,128)(2,1)S(1)}, u32[]{:S(2)}, u32[]{:S(2)}) collective-permute-start(bf16[1,2,2,256,256]{4,3,2,1,0:T(8,128)(2,1)S(1)} %pad_maximum_fusion.1), channel_id=1, source_target_pairs={{0,1},{1,2},{2,3},{3,4},{4,5},{5,6},{6,7},{8,9},{9,10},{10,11},{11... | collective-permute-start | bytes 1572872 | tf_op jit(solution)/shard_map/ppermute | solution.py:37
  43.4 24.5 %collective-permute-start.4 = (bf16[1,2,2,256,256]{4,3,2,1,0:T(8,128)(2,1)S(1)}, bf16[1,2,2,256,256]{4,3,2,1,0:T(8,128)(2,1)S(1)}, u32[]{:S(2)}, u32[]{:S(2)}) collective-permute-start(bf16[1,2,2,256,256]{4,3,2,1,0:T(8,128)(2,1)S(1)} %pad_maximum_fusion.1), channel_id=1, source_target_pairs={{1,0},{2,1},{3,2},{4,3},{5,4},{6,5},{7,6},{9,8},{10,9},{11,10},{12... | collective-permute-start | bytes 1572872 | tf_op jit(solution)/shard_map/ppermute | solution.py:38
  72.3 27.0 %collective-permute-start.6 = (bf16[1,1,2,2,256,256]{5,4,3,2,1,0:T(8,128)(2,1)S(1)}, bf16[1,1,2,2,256,256]{5,4,3,2,1,0:T(8,128)(2,1)S(1)}, u32[]{:S(2)}, u32[]{:S(2)}) collective-permute-start(bf16[1,1,2,2,256,256]{5,4,3,2,1,0:T(8,128)(2,1)S(1)} %pad_maximum_fusion.3), channel_id=1, source_target_pairs={{1,0},{2,1},{3,2},{4,3},{5,4},{6,5},{7,6},{9,8},{10,9},{11,10},{12... | collective-permute-start | bytes 1572872 | tf_op jit(solution)/shard_map/ppermute | solution.py:46
  75.6 25.3 %collective-permute-start.5 = (bf16[1,1,2,2,256,256]{5,4,3,2,1,0:T(8,128)(2,1)S(1)}, bf16[1,1,2,2,256,256]{5,4,3,2,1,0:T(8,128)(2,1)S(1)}, u32[]{:S(2)}, u32[]{:S(2)}) collective-permute-start(bf16[1,1,2,2,256,256]{5,4,3,2,1,0:T(8,128)(2,1)S(1)} %pad_maximum_fusion.2), channel_id=1, source_target_pairs={{0,1},{1,2},{2,3},{3,4},{4,5},{5,6},{6,7},{8,9},{9,10},{10,11},{11... | collective-permute-start | bytes 1572872 | tf_op jit(solution)/shard_map/ppermute | solution.py:46
